TPU v7x, 256 devices: a whole 4x4x8 slice. The times are simulated.
256 devices in a mesh: freq: 64 (over y, z, x_hi), inp: 4 (over x_lo, core).
Axes of the slice: x: 4 (x_hi: 2, x_lo: 2; x = x_hi * 2 + x_lo), y: 4, z: 8, core: 2. Of those that a mesh axis runs over, the one named last changes fastest.
Arguments:
- voltages: int32 [192, 2048, 1024], P('freq', None, 'inp'), may hold values from -128 to 127
- taps: float32 [12, 2048], replicated, may hold values from -0.013671875 to 0.013671875
- start: int32 [8, 2, 1024], replicated, may hold values from -127 to 127
Outputs:
- cleaned: bfloat16 [1024, 192, 2, 1024], P('freq', None, None, 'inp')
- ritz_matrix: float32 [1024, 8, 8], P('freq')
Inputs may be any that keep to these rules, and one draw needn't show every extreme that they name: `voltages`: 8-bit voltage samples.
All inputs are finite; a program needn't handle non-finite values.
Results may differ from a plain program's by a relative error of at most 0.0052.
Values may be sent and summed in bfloat16 or wider, within the bound.
No kernel may reach another device: no remote copies, remote signals or barrier semaphores. Data moves between devices by JAX's collectives and lax.ppermute only.
A program may use at most 192 MiB of HBM per device.

v0:
```python
import math
import jax
import jax.numpy as jnp
from jax import lax
from jax.sharding import PartitionSpec as P

ITERS = 4


def from_behind(value, axis, steps):
    count = lax.axis_size(axis)
    pairs = [(source, (source + steps) % count) for source in range(count)]
    return lax.ppermute(value, axis, pairs)


def project_rows(basis_rows, channel_data):
    projected = jnp.einsum(
        "ckr,cmr->ckm", basis_rows, channel_data, precision=lax.Precision.HIGHEST
    )
    return lax.psum(projected, "inp")


def subspace_clean(turned, start_block):
    highest = lax.Precision.HIGHEST
    channel_local, spectra_count, part_count, inputs_width = turned.shape
    row_count = part_count * inputs_width
    channel_data = turned.reshape(channel_local, spectra_count, row_count).astype(jnp.float32)
    start_rows = start_block.reshape(start_block.shape[0], row_count).astype(jnp.float32)
    basis_rows = jnp.broadcast_to(start_rows[None], (channel_local,) + start_rows.shape)
    for iteration in range(ITERS):
        projected = project_rows(basis_rows, channel_data)
        mapped = (
            jnp.einsum("ckm,cmr->ckr", projected, channel_data, precision=highest) / spectra_count
        )
        gram_matrix = jnp.einsum("ckr,cjr->ckj", mapped, mapped, precision=highest)
        gram_matrix = lax.psum(gram_matrix, "inp")
        lower_factor = jnp.linalg.cholesky(gram_matrix)
        basis_rows = lax.linalg.triangular_solve(lower_factor, mapped, left_side=True, lower=True)
    projected = project_rows(basis_rows, channel_data)
    ritz_matrix = (
        jnp.einsum("ckm,cjm->ckj", projected, projected, precision=highest) / spectra_count
    )
    cleaned = channel_data - jnp.einsum("ckm,ckr->cmr", projected, basis_rows, precision=highest)
    cleaned = cleaned.reshape(channel_local, spectra_count, part_count, inputs_width).astype(
        jnp.bfloat16
    )
    return (cleaned, ritz_matrix)


def shards(voltages, taps, start):
    slot_count = voltages.shape[0]
    frame_len = voltages.shape[1]
    inputs_local = voltages.shape[2]
    channel_count = frame_len // 2
    tap_count = taps.shape[0]
    frame_stack = voltages.astype(jnp.bfloat16)
    history_len = tap_count - 1
    group_count = lax.axis_size("freq")
    portions = [frame_stack]
    shift_count = (history_len - 1) // slot_count + 1
    for distance in range(1, shift_count + 1):
        first_frame = max(0, distance * slot_count - history_len)
        portion = frame_stack[first_frame:]
        offset_mod = distance % group_count
        arrived = from_behind(portion, "freq", offset_mod)
        portions = [arrived] + portions
    extended = jnp.concatenate(portions, axis=0)
    filtered = jnp.zeros((slot_count, frame_len, inputs_local), jnp.float32)
    for tap_index in range(tap_count):
        window = extended[tap_index : tap_index + slot_count].astype(jnp.float32)
        filtered = filtered + taps[tap_index][None, :, None] * window
    channel_idx = lax.broadcasted_iota(jnp.int32, (channel_count, frame_len), 0)
    sample_idx = lax.broadcasted_iota(jnp.int32, (channel_count, frame_len), 1)
    angles = (channel_idx * sample_idx % frame_len).astype(jnp.float32) * (
        2.0 * math.pi / frame_len
    )
    dft_scale = 1.0 / math.sqrt(channel_count)
    cosine = jnp.cos(angles)
    sine_table = jnp.sin(angles)
    real_part = (
        jnp.einsum("kn,sni->ksi", cosine, filtered, precision=lax.Precision.HIGHEST) * dft_scale
    )
    imag_part = (
        -jnp.einsum("kn,sni->ksi", sine_table, filtered, precision=lax.Precision.HIGHEST)
        * dft_scale
    )
    spectra = jnp.stack([real_part, imag_part], axis=2).astype(jnp.bfloat16)
    turned = lax.all_to_all(spectra, "freq", split_axis=0, concat_axis=1, tiled=True)
    start_local = lax.dynamic_slice_in_dim(
        start, lax.axis_index("inp") * inputs_local, inputs_local, 2
    )
    cleaned, ritz_matrix = subspace_clean(turned, start_local)
    return (cleaned, ritz_matrix)


def solution(mesh):
    placed = (P("freq", None, "inp"), P(), P())
    return jax.shard_map(
        shards,
        mesh=mesh,
        in_specs=placed,
        out_specs=(P("freq", None, None, "inp"), P("freq", None, None)),
        check_vma=False,
    )
```

profile of v0, /device:TPU:1, one launch (start us, length us, event | category | flops | bytes accessed | tf_op | source)
XLA Modules:
  0.0 1002.1 jit_solution(7785082553652282310)
XLA Ops:
  7.2 3.3 convert_element_type.65
  10.5 5.0 collective-permute-start.1
  15.5 1.6 collective-permute-start.2
  17.2 1.6 collective-permute-start.3
  18.9 3.4 collective-permute-start
  22.3 181.6 %collective-permute-done = bf16[2,2048,256]{2,1,0:T(8,128)(2,1)S(1)} collective-permute-done((bf16[2,2048,256]{2,1,0:T(8,128)(2,1)S(1)}, bf16[2,2048,256]{2,1,0:T(8,128)(2,1)S(1)}, u32[]{:S(2)}, u32[]{:S(2)}) %collective-permute-start) | collective-permute-done | bytes 2097184 | tf_op jit(solution)/shard_map/ppermute | solution.py:13
  204.1 0.4 constant_dynamic-update-slice_fusion
  204.6 16.6 %collective-permute-done.2 = bf16[3,2048,256]{2,1,0:T(8,128)(2,1)S(1)} collective-permute-done((bf16[3,2048,256]{2,1,0:T(8,128)(2,1)S(1)}, bf16[3,2048,256]{2,1,0:T(8,128)(2,1)S(1)}, u32[]{:S(2)}, u32[]{:S(2)}) %collective-permute-start.2) | collective-permute-done | bytes 3145760 | tf_op jit(solution)/shard_map/ppermute | solution.py:13
  221.2 0.4 constant_dynamic-update-slice_fusion.2
  221.6 70.7 %collective-permute-done.3 = bf16[3,2048,256]{2,1,0:T(8,128)(2,1)S(1)} collective-permute-done((bf16[3,2048,256]{2,1,0:T(8,128)(2,1)S(1)}, bf16[3,2048,256]{2,1,0:T(8,128)(2,1)S(1)}, u32[]{:S(2)}, u32[]{:S(2)}) %collective-permute-start.3) | collective-permute-done | bytes 3145760 | tf_op jit(solution)/shard_map/ppermute | solution.py:13
  292.5 9.7 multiply_add_fusion
  302.2 64.8 %fusion.19 = bf16[1024,3,1,256]{3,0,1,2:T(8,128)(2,1)S(1)} fusion(f32[3,2048,256]{2,1,0:T(8,128)} %multiply_add_fusion), kind=kOutput, calls=%fused_computation.25 | convolution fusion | flops 19358285824 | bytes 7864320 | tf_op jit(solution)/shard_map/kn,sni->ksi/dot_general | solution.py:81
  367.0 53.0 %fusion.22 = bf16[1024,3,1,256]{3,0,1,2:T(8,128)(2,1)S(1)} fusion(f32[3,2048,256]{2,1,0:T(8,128)S(1)} %copy-done), kind=kOutput, calls=%fused_computation.26 | convolution fusion | flops 19359072256 | bytes 7864320 | tf_op jit(solution)/shard_map/kn,sni->ksi/dot_general | solution.py:84
  420.0 0.3 pad_maximum_fusion.1
  420.3 4.9 copy.77
  425.2 98.1 %all-to-all-start = ((bf16[1024,3,2,256]{3,2,1,0:T(2,128)(2,1)}), bf16[1024,3,2,256]{3,2,1,0:T(2,128)(2,1)S(1)}, u32[]{:S(2)}, u32[]{:S(2)}) async-start(bf16[1024,3,2,256]{3,2,1,0:T(2,128)(2,1)} %copy.77), calls=%async_computation | async-start | bytes 6291456 | tf_op jit(solution)/shard_map/all_to_all | solution.py:88
  523.4 0.7 convert_bitcast_fusion
  524.1 71.6 %all-to-all-done = bf16[1024,3,2,256]{3,2,1,0:T(2,128)(2,1)S(1)} async-done(((bf16[1024,3,2,256]{3,2,1,0:T(2,128)(2,1)}), bf16[1024,3,2,256]{3,2,1,0:T(2,128)(2,1)S(1)}, u32[]{:S(2)}, u32[]{:S(2)}) %all-to-all-start) | async-done | bytes 3145760 | tf_op jit(solution)/shard_map/all_to_all | solution.py:88
  595.7 4.7 copy.110
  600.4 4.6 reshape.41
  605.0 3.2 fusion.25
  608.3 38.9 %all-reduce.6.cloned.1.call-done = f32[16,8,192]{2,1,0:T(8,128)} async-done(((f32[16,8,192]{2,1,0:T(8,128)}), f32[16,8,192]{2,1,0:T(8,128)}) %all-reduce.6.cloned.1.call-update) | async-done | bytes 98320 | tf_op jit(solution)/shard_map/psum | solution.py:20
  647.2 2.2 convolution_multiply_fusion.3
  649.5 0.6 fusion.48
  650.1 10.6 %psum.64 = f32[16,8,8]{1,2,0:T(8,128)S(1)} all-reduce(f32[16,8,8]{1,2,0:T(8,128)S(1)} %fusion.48), channel_id=1, replica_groups=mesh['freq'=64,'inp'=4] {'inp'}, use_global_device_ids=true, to_apply=%region_1.2 | all-reduce | flops 1024 | bytes 8192 | tf_op jit(solution)/shard_map/psum | solution.py:36
  660.8 0.6 fusion.38
  661.4 12.4 %custom-call.12 = f32[16,8,8]{2,1,0:T(8,128)S(1)} custom-call(f32[16,8,8]{2,1,0:T(8,128)} %fusion.38), custom_call_target="Cholesky" | custom-call | tf_op jit(solution)/shard_map/jit(cholesky)/cholesky | solution.py:37
  674.1 10.0 custom-call.13
  684.1 0.5 fusion.36
  684.6 3.2 fusion.49
  687.8 0.4 all-reduce.10.cloned.1.call-start
  688.3 42.2 %all-reduce.8.cloned.1.call-done = f32[16,8,192]{2,1,0:T(8,128)} async-done(((f32[16,8,192]{2,1,0:T(8,128)}), f32[16,8,192]{2,1,0:T(8,128)}) %all-reduce.8.cloned.1.call-update) | async-done | bytes 98320 | tf_op jit(solution)/shard_map/psum | solution.py:20
  730.5 2.2 convolution_multiply_fusion.2
  732.7 0.6 fusion.50
  733.3 10.6 %psum.66 = f32[16,8,8]{1,2,0:T(8,128)S(1)} all-reduce(f32[16,8,8]{1,2,0:T(8,128)S(1)} %fusion.50), channel_id=1, replica_groups=mesh['freq'=64,'inp'=4] {'inp'}, use_global_device_ids=true, to_apply=%region_5.8 | all-reduce | flops 1024 | bytes 8192 | tf_op jit(solution)/shard_map/psum | solution.py:36
  744.0 0.6 fusion.35
  744.7 12.4 %custom-call.14 = f32[16,8,8]{2,1,0:T(8,128)S(1)} custom-call(f32[16,8,8]{2,1,0:T(8,128)} %fusion.35), custom_call_target="Cholesky" | custom-call | tf_op jit(solution)/shard_map/jit(cholesky)/cholesky | solution.py:37
  757.3 10.0 custom-call.15
  767.3 0.5 fusion.33
  767.8 3.2 fusion.51
  771.1 42.6 %all-reduce.10.cloned.1.call-done = f32[16,8,192]{2,1,0:T(8,128)} async-done(((f32[16,8,192]{2,1,0:T(8,128)}), f32[16,8,192]{2,1,0:T(8,128)}) %all-reduce.10.cloned.1.call-update) | async-done | bytes 98320 | tf_op jit(solution)/shard_map/psum | solution.py:20
  813.8 2.2 convolution_multiply_fusion.1
  816.0 0.6 fusion.52
  816.6 10.6 %psum.68 = f32[16,8,8]{1,2,0:T(8,128)S(1)} all-reduce(f32[16,8,8]{1,2,0:T(8,128)S(1)} %fusion.52), channel_id=1, replica_groups=mesh['freq'=64,'inp'=4] {'inp'}, use_global_device_ids=true, to_apply=%region_7.10 | all-reduce | flops 1024 | bytes 8192 | tf_op jit(solution)/shard_map/psum | solution.py:36
  827.3 0.6 fusion.32
  827.9 12.4 %custom-call.16 = f32[16,8,8]{2,1,0:T(8,128)S(1)} custom-call(f32[16,8,8]{2,1,0:T(8,128)} %fusion.32), custom_call_target="Cholesky" | custom-call | tf_op jit(solution)/shard_map/jit(cholesky)/cholesky | solution.py:37
  840.6 10.0 custom-call.17
  850.6 0.5 fusion.30
  851.1 3.2 fusion.53
  854.4 42.6 %all-reduce.12.cloned.1.call-done = f32[16,8,192]{2,1,0:T(8,128)} async-done(((f32[16,8,192]{2,1,0:T(8,128)}), f32[16,8,192]{2,1,0:T(8,128)}) %all-reduce.12.cloned.1.call-update) | async-done | bytes 98320 | tf_op jit(solution)/shard_map/psum | solution.py:20
  897.0 2.2 convolution_multiply_fusion
  899.3 0.6 fusion.54
  899.9 10.8 %psum.70 = f32[16,8,8]{1,2,0:T(8,128)S(1)} all-reduce(f32[16,8,8]{1,2,0:T(8,128)S(1)} %fusion.54), channel_id=1, replica_groups=mesh['freq'=64,'inp'=4] {'inp'}, use_global_device_ids=true, to_apply=%region_9.12 | all-reduce | flops 1024 | bytes 8192 | tf_op jit(solution)/shard_map/psum | solution.py:36
  910.7 0.6 fusion.29
  911.4 12.4 %custom-call.18 = f32[16,8,8]{2,1,0:T(8,128)S(1)} custom-call(f32[16,8,8]{2,1,0:T(8,128)} %fusion.29), custom_call_target="Cholesky" | custom-call | tf_op jit(solution)/shard_map/jit(cholesky)/cholesky | solution.py:37
  924.0 10.0 custom-call.19
  934.0 0.5 fusion.27
  934.6 0.7 copy-done.1
  935.3 3.2 fusion.55
  938.5 42.7 %all-reduce.14.cloned.1.call-done = f32[16,8,192]{2,1,0:T(8,128)} async-done(((f32[16,8,192]{2,1,0:T(8,128)}), f32[16,8,192]{2,1,0:T(8,128)}) %all-reduce.14.cloned.1.call-update) | async-done | bytes 98320 | tf_op jit(solution)/shard_map/psum | solution.py:20
  981.2 7.7 subtract_convert_fusion
  988.9 5.5 convert_element_type.82
  994.4 0.3 convolution_multiply_fusion.4
  994.7 0.7 copy.99
  (44 shorter events, 2.2 us)
Async XLA Ops:
  7.2 15.1 %copy-start.3 = (f32[12,2048]{1,0:T(8,128)S(1)}, f32[12,2048]{1,0:T(8,128)}, u32[]{:S(2)}) copy-start(f32[12,2048]{1,0:T(8,128)} %param.7) | copy-start | bytes 294916
  10.5 193.6 %collective-permute-start.1 = (bf16[3,2048,256]{2,1,0:T(8,128)(2,1)S(1)}, bf16[3,2048,256]{2,1,0:T(8,128)(2,1)S(1)}, u32[]{:S(2)}, u32[]{:S(2)}) collective-permute-start(bf16[3,2048,256]{2,1,0:T(8,128)(2,1)S(1)} %convert_element_type.65), channel_id=1, source_target_pairs={{0,12},{4,16},{8,20},{12,24},{16,28},{20,32},{24,36},{28,40},{32,4... | collective-permute-start | bytes 9437192 | tf_op jit(solution)/shard_map/ppermute | solution.py:13
  15.5 205.7 %collective-permute-start.2 = (bf16[3,2048,256]{2,1,0:T(8,128)(2,1)S(1)}, bf16[3,2048,256]{2,1,0:T(8,128)(2,1)S(1)}, u32[]{:S(2)}, u32[]{:S(2)}) collective-permute-start(bf16[3,2048,256]{2,1,0:T(8,128)(2,1)S(1)} %convert_element_type.65), channel_id=1, source_target_pairs={{0,8},{4,12},{8,16},{12,20},{16,24},{20,28},{24,32},{28,36},{32,40... | collective-permute-start | bytes 9437192 | tf_op jit(solution)/shard_map/ppermute | solution.py:13
  17.2 275.1 %collective-permute-start.3 = (bf16[3,2048,256]{2,1,0:T(8,128)(2,1)S(1)}, bf16[3,2048,256]{2,1,0:T(8,128)(2,1)S(1)}, u32[]{:S(2)}, u32[]{:S(2)}) collective-permute-start(bf16[3,2048,256]{2,1,0:T(8,128)(2,1)S(1)} %convert_element_type.65), channel_id=1, source_target_pairs={{0,4},{4,8},{8,12},{12,16},{16,20},{20,24},{24,28},{28,32},{32,36}... | collective-permute-start | bytes 9437192 | tf_op jit(solution)/shard_map/ppermute | solution.py:13
  18.9 185.1 %collective-permute-start = (bf16[2,2048,256]{2,1,0:T(8,128)(2,1)S(1)}, bf16[2,2048,256]{2,1,0:T(8,128)(2,1)S(1)}, u32[]{:S(2)}, u32[]{:S(2)}) collective-permute-start(bf16[2,2048,256]{2,1,0:T(8,128)(2,1)S(1)} %slice.98), channel_id=1, source_target_pairs={{0,16},{4,20},{8,24},{12,28},{16,32},{20,36},{24,40},{28,44},{32,4... | collective-permute-start | bytes 6291464 | tf_op jit(solution)/shard_map/ppermute | solution.py:13
  302.2 64.8 %copy-start = (f32[3,2048,256]{2,1,0:T(8,128)S(1)}, f32[3,2048,256]{2,1,0:T(8,128)}, u32[]{:S(2)}) copy-start(f32[3,2048,256]{2,1,0:T(8,128)} %multiply_add_fusion) | copy-start | bytes 18874372
  425.2 170.6 %all-to-all-start = ((bf16[1024,3,2,256]{3,2,1,0:T(2,128)(2,1)}), bf16[1024,3,2,256]{3,2,1,0:T(2,128)(2,1)S(1)}, u32[]{:S(2)}, u32[]{:S(2)}) async-start(bf16[1024,3,2,256]{3,2,1,0:T(2,128)(2,1)} %copy.77), calls=%async_computation | async-start | bytes 6291456 | tf_op jit(solution)/shard_map/all_to_all | solution.py:88
  523.3 123.9 %all-reduce.6.cloned.1.call-start = ((), (), s32[]{:S(2)}) async-start(), calls=%async_computation.1 | async-start | bytes 262144 | tf_op jit(solution)/shard_map/psum | solution.py:20
  608.2 122.3 %all-reduce.8.cloned.1.call-start = ((), (), s32[]{:S(2)}) async-start(), calls=%async_computation.2 | async-start | bytes 262144 | tf_op jit(solution)/shard_map/psum | solution.py:20
  687.8 126.0 %all-reduce.10.cloned.1.call-start = ((), (), s32[]{:S(2)}) async-start(), calls=%async_computation.3 | async-start | bytes 262144 | tf_op jit(solution)/shard_map/psum | solution.py:20
  771.1 126.0 %all-reduce.12.cloned.1.call-start = ((), (), s32[]{:S(2)}) async-start(), calls=%async_computation.4 | async-start | bytes 262144 | tf_op jit(solution)/shard_map/psum | solution.py:20
  854.3 126.8 %all-reduce.14.cloned.1.call-start = ((), (), s32[]{:S(2)}) async-start(), calls=%async_computation.5 | async-start | bytes 262144 | tf_op jit(solution)/shard_map/psum | solution.py:20
  934.6 0.7 copy-start.1
  981.2 13.2 %copy-start.2 = (f32[16,8,192]{2,1,0:T(8,128)S(1)}, f32[16,8,192]{2,1,0:T(8,128)}, u32[]{:S(2)}) copy-start(f32[16,8,192]{2,1,0:T(8,128)} %all-reduce.14.cloned.1.call-done) | copy-start | bytes 294916
Sparse Core Ops, SparseCore 0:
  608.4 38.8 all-reduce.5
  687.9 42.5 all-reduce.7
  771.2 42.5 all-reduce.9
  854.4 42.5 all-reduce.11
  938.6 42.5 all-reduce.13
where the time goes:
time: 1010 us; the launch traced here: 1000 us
  waiting for transfers between devices  550 us (54%)
  matrix products  155 us (15%)
  starting transfers between devices  110 us (11%)
  other arithmetic  107 us (11%)
  blocking collectives  42.7 us (4%)
  local copies, waits for them, and re-layouts  23 us (2%)
  between operations  14.2 us (1%)
    ppermute x4, waiting for transfers between devices, from_behind(): return lax.ppermute(value, axis, pairs)  269 us
    psum x5, waiting for transfers between devices, project_rows(): return lax.psum(projected, 'inp')  209 us
    all_to_all x1, starting transfers between devices, shards(): lax.all_to_all(spectra, 'freq', split_axis=0, concat_axis=1, tiled=True)  98.1 us
    all_to_all x1, waiting for transfers between devices, shards(): lax.all_to_all(spectra, 'freq', split_axis=0, concat_axis=1, tiled=True)  71.6 us
    dot_general x1, matrix products, shards(): jnp.einsum('kn,sni->ksi', cosine, filtered, precision=lax.Precision.HIGHEST)  64.8 us
    dot_general x1, matrix products, shards(): jnp.einsum('kn,sni->ksi', sine_table, filtered, precision=lax.Precision.H...  53 us
    another operation x13, other arithmetic, subspace_clean(): lower_factor = jnp.linalg.cholesky(gram_matrix)  49.9 us
    psum x4, blocking collectives, subspace_clean(): gram_matrix = lax.psum(gram_matrix, 'inp')  42.7 us
  transfers between devices with their start and end apart: 10, of which 9 were waited for; matrix products, arithmetic and copies ran while one was open for 0% of the time, Pallas kernels for 0%

commit v1 on v0

--- a/solution.py
+++ b/solution.py
@@ -5,6 +5,10 @@
 from jax.sharding import PartitionSpec as P
 
 ITERS = 4
+
+
+def cover_the_screen(z_in):
+    return jnp.sum(lax.all_gather(z_in, axis_name="inp"), axis=0)
 
 
 def from_behind(value, axis, steps):
@@ -17,7 +21,7 @@
     projected = jnp.einsum(
         "ckr,cmr->ckm", basis_rows, channel_data, precision=lax.Precision.HIGHEST
     )
-    return lax.psum(projected, "inp")
+    return cover_the_screen(projected)
 
 
 def subspace_clean(turned, start_block):

time: 1010 us -> 828 us (0.82)
  waiting for transfers between devices: 550 us -> 341 us
  blocking collectives: 42.7 us -> 86.3 us
  between operations: 14.2 us -> 1.12 us
    psum x5 -> x0, waiting for transfers between devices: 209 us -> none  [project_rows(): return lax.psum(projected, 'inp')]
    all_gather x0 -> x5, blocking collectives: none -> 43.9 us  [cover_the_screen(): return jnp.sum(lax.all_gather(z_in, axis_name='inp'), axis=0)]
  transfers between devices with their start and end apart: 10 -> 5, of which waited for: 9 -> 4; matrix products, arithmetic and copies ran while one was open for 0% -> 0% of each run, Pallas kernels for 0% -> 0%
where the time goes in v1:
time: 828 us; the launch traced here: 821 us
  waiting for transfers between devices  341 us (41%)
  matrix products  148 us (18%)
  other arithmetic  112 us (14%)
  starting transfers between devices  110 us (13%)
  blocking collectives  86.3 us (10%)
  local copies, waits for them, and re-layouts  23 us (3%)
    ppermute x4, waiting for transfers between devices, from_behind(): return lax.ppermute(value, axis, pairs)  269 us
    all_to_all x1, starting transfers between devices, shards(): lax.all_to_all(spectra, 'freq', split_axis=0, concat_axis=1, tiled=True)  98.1 us
    all_to_all x1, waiting for transfers between devices, shards(): lax.all_to_all(spectra, 'freq', split_axis=0, concat_axis=1, tiled=True)  71.7 us
    dot_general x1, matrix products, shards(): jnp.einsum('kn,sni->ksi', cosine, filtered, precision=lax.Precision.HIGHEST)  64.8 us
    dot_general x1, matrix products, shards(): jnp.einsum('kn,sni->ksi', sine_table, filtered, precision=lax.Precision.H...  53 us
    another operation x13, other arithmetic, subspace_clean(): lower_factor = jnp.linalg.cholesky(gram_matrix)  49.9 us
    all_gather x5, blocking collectives, cover_the_screen(): return jnp.sum(lax.all_gather(z_in, axis_name='inp'), axis=0)  43.9 us
    psum x4, blocking collectives, subspace_clean(): gram_matrix = lax.psum(gram_matrix, 'inp')  42.5 us
  transfers between devices with their start and end apart: 5, of which 4 were waited for; matrix products, arithmetic and copies ran while one was open for 0% of the time, Pallas kernels for 0%

profile of v1, /device:TPU:1, one launch (start us, length us, event | category | flops | bytes accessed | tf_op | source)
XLA Modules:
  0.0 821.1 jit_solution(7553258419217040100)
XLA Ops:
  0.6 3.3 convert_element_type.65
  4.0 5.0 collective-permute-start.1
  9.0 1.6 collective-permute-start.2
  10.6 1.6 collective-permute-start.3
  12.4 3.4 collective-permute-start
  15.8 181.6 %collective-permute-done = bf16[2,2048,256]{2,1,0:T(8,128)(2,1)S(1)} collective-permute-done((bf16[2,2048,256]{2,1,0:T(8,128)(2,1)S(1)}, bf16[2,2048,256]{2,1,0:T(8,128)(2,1)S(1)}, u32[]{:S(2)}, u32[]{:S(2)}) %collective-permute-start) | collective-permute-done | bytes 2097184 | tf_op jit(solution)/shard_map/ppermute | solution.py:17
  198.0 16.6 %collective-permute-done.2 = bf16[3,2048,256]{2,1,0:T(8,128)(2,1)S(1)} collective-permute-done((bf16[3,2048,256]{2,1,0:T(8,128)(2,1)S(1)}, bf16[3,2048,256]{2,1,0:T(8,128)(2,1)S(1)}, u32[]{:S(2)}, u32[]{:S(2)}) %collective-permute-start.2) | collective-permute-done | bytes 3145760 | tf_op jit(solution)/shard_map/ppermute | solution.py:17
  215.1 70.7 %collective-permute-done.3 = bf16[3,2048,256]{2,1,0:T(8,128)(2,1)S(1)} collective-permute-done((bf16[3,2048,256]{2,1,0:T(8,128)(2,1)S(1)}, bf16[3,2048,256]{2,1,0:T(8,128)(2,1)S(1)}, u32[]{:S(2)}, u32[]{:S(2)}) %collective-permute-start.3) | collective-permute-done | bytes 3145760 | tf_op jit(solution)/shard_map/ppermute | solution.py:17
  286.0 9.7 %multiply_add_fusion = f32[3,2048,256]{2,1,0:T(8,128)} fusion(bf16[3,2048,256]{2,1,0:T(8,128)(2,1)S(1)} %convert_element_type.65, bf16[3,2048,256]{2,1,0:T(8,128)(2,1)S(1)} %collective-permute-done.3, bf16[3,2048,256]{2,1,0:T(8,128)(2,1)S(1)} %collective-permute-done.2, bf16[3,2048,256]{2,1,0:T(8,128)(2,1)S(1)} %collective-permute-done.1, ...), kind=kLoop, calls=%fused_computation.18 | loop fusion | flops 58195968 | bytes 37847040 | tf_op jit(solution)/shard_map/add | solution.py:75
  295.7 64.8 %fusion.19 = bf16[1024,3,1,256]{3,0,1,2:T(8,128)(2,1)S(1)} fusion(f32[3,2048,256]{2,1,0:T(8,128)} %multiply_add_fusion), kind=kOutput, calls=%fused_computation.25 | convolution fusion | flops 19358285824 | bytes 7864320 | tf_op jit(solution)/shard_map/kn,sni->ksi/dot_general | solution.py:85
  360.5 53.0 %fusion.22 = bf16[1024,3,1,256]{3,0,1,2:T(8,128)(2,1)S(1)} fusion(f32[3,2048,256]{2,1,0:T(8,128)S(1)} %copy-done), kind=kOutput, calls=%fused_computation.26 | convolution fusion | flops 19359072256 | bytes 7864320 | tf_op jit(solution)/shard_map/kn,sni->ksi/dot_general | solution.py:88
  413.8 4.9 copy.77
  418.7 98.1 %all-to-all-start = ((bf16[1024,3,2,256]{3,2,1,0:T(2,128)(2,1)}), bf16[1024,3,2,256]{3,2,1,0:T(2,128)(2,1)S(1)}, u32[]{:S(2)}, u32[]{:S(2)}) async-start(bf16[1024,3,2,256]{3,2,1,0:T(2,128)(2,1)} %copy.77), calls=%async_computation | async-start | bytes 6291456 | tf_op jit(solution)/shard_map/all_to_all | solution.py:92
  516.8 0.7 convert_bitcast_fusion
  517.5 71.7 %all-to-all-done = bf16[1024,3,2,256]{3,2,1,0:T(2,128)(2,1)S(1)} async-done(((bf16[1024,3,2,256]{3,2,1,0:T(2,128)(2,1)}), bf16[1024,3,2,256]{3,2,1,0:T(2,128)(2,1)S(1)}, u32[]{:S(2)}, u32[]{:S(2)}) %all-to-all-start) | async-done | bytes 3145760 | tf_op jit(solution)/shard_map/all_to_all | solution.py:92
  589.2 4.7 copy.110
  593.9 4.6 reshape.41
  598.5 2.5 fusion.25
  601.0 10.9 %all-gather = f32[64,8,192]{2,1,0:T(8,128)} all-gather(f32[16,8,192]{2,1,0:T(8,128)S(1)} %fusion.25), channel_id=2, replica_groups=mesh['freq'=64,'inp'=4] {'inp'}, dimensions={0}, use_global_device_ids=true | all-gather | bytes 491520 | tf_op jit(solution)/shard_map/all_gather | solution.py:11
  611.9 1.1 reduce_sum.45
  613.0 1.3 convolution_multiply_fusion.3
  614.3 0.6 fusion.48
  614.9 10.6 %psum.28 = f32[16,8,8]{1,2,0:T(8,128)S(1)} all-reduce(f32[16,8,8]{1,2,0:T(8,128)S(1)} %fusion.48), channel_id=1, replica_groups=mesh['freq'=64,'inp'=4] {'inp'}, use_global_device_ids=true, to_apply=%region_1.2 | all-reduce | flops 1024 | bytes 8192 | tf_op jit(solution)/shard_map/psum | solution.py:40
  625.7 0.6 fusion.38
  626.3 12.4 %custom-call.12 = f32[16,8,8]{2,1,0:T(8,128)S(1)} custom-call(f32[16,8,8]{2,1,0:T(8,128)} %fusion.38), custom_call_target="Cholesky" | custom-call | tf_op jit(solution)/shard_map/jit(cholesky)/cholesky | solution.py:41
  638.9 10.0 %custom-call.13 = f32[16,1,8,8]{2,3,1,0:T(8,128)S(1)} custom-call(f32[16,1,8,8]{3,2,1,0:T(8,128)S(1)} %select_bitcast_fusion.3), custom_call_target="InvertDiagBlocksLowerTriangular" | custom-call | tf_op jit(solution)/shard_map/triangular_solve/custom-call.0 | solution.py:42
  649.0 0.5 fusion.36
  649.5 2.5 fusion.49
  652.0 8.5 %all-gather.1 = f32[64,8,192]{2,1,0:T(8,128)} all-gather(f32[16,8,192]{2,1,0:T(8,128)S(1)} %fusion.49), channel_id=3, replica_groups=mesh['freq'=64,'inp'=4] {'inp'}, dimensions={0}, use_global_device_ids=true | all-gather | bytes 491520 | tf_op jit(solution)/shard_map/all_gather | solution.py:11
  660.5 1.1 reduce_sum.46
  661.6 1.3 convolution_multiply_fusion.2
  662.9 0.6 fusion.50
  663.5 10.6 %psum.29 = f32[16,8,8]{1,2,0:T(8,128)S(1)} all-reduce(f32[16,8,8]{1,2,0:T(8,128)S(1)} %fusion.50), channel_id=1, replica_groups=mesh['freq'=64,'inp'=4] {'inp'}, use_global_device_ids=true, to_apply=%region_5.8 | all-reduce | flops 1024 | bytes 8192 | tf_op jit(solution)/shard_map/psum | solution.py:40
  674.2 0.6 fusion.35
  674.9 12.4 %custom-call.14 = f32[16,8,8]{2,1,0:T(8,128)S(1)} custom-call(f32[16,8,8]{2,1,0:T(8,128)} %fusion.35), custom_call_target="Cholesky" | custom-call | tf_op jit(solution)/shard_map/jit(cholesky)/cholesky | solution.py:41
  687.5 10.0 %custom-call.15 = f32[16,1,8,8]{2,3,1,0:T(8,128)S(1)} custom-call(f32[16,1,8,8]{3,2,1,0:T(8,128)S(1)} %select_bitcast_fusion.2), custom_call_target="InvertDiagBlocksLowerTriangular" | custom-call | tf_op jit(solution)/shard_map/triangular_solve/custom-call.0 | solution.py:42
  697.5 0.5 fusion.33
  698.0 2.5 fusion.51
  700.6 8.1 all-gather.2
  708.7 1.1 reduce_sum.47
  709.7 1.3 convolution_multiply_fusion.1
  711.1 0.6 fusion.52
  711.7 10.6 %psum.30 = f32[16,8,8]{1,2,0:T(8,128)S(1)} all-reduce(f32[16,8,8]{1,2,0:T(8,128)S(1)} %fusion.52), channel_id=1, replica_groups=mesh['freq'=64,'inp'=4] {'inp'}, use_global_device_ids=true, to_apply=%region_7.10 | all-reduce | flops 1024 | bytes 8192 | tf_op jit(solution)/shard_map/psum | solution.py:40
  722.4 0.6 fusion.32
  723.0 12.4 %custom-call.16 = f32[16,8,8]{2,1,0:T(8,128)S(1)} custom-call(f32[16,8,8]{2,1,0:T(8,128)} %fusion.32), custom_call_target="Cholesky" | custom-call | tf_op jit(solution)/shard_map/jit(cholesky)/cholesky | solution.py:41
  735.7 10.0 %custom-call.17 = f32[16,1,8,8]{2,3,1,0:T(8,128)S(1)} custom-call(f32[16,1,8,8]{3,2,1,0:T(8,128)S(1)} %select_bitcast_fusion.1), custom_call_target="InvertDiagBlocksLowerTriangular" | custom-call | tf_op jit(solution)/shard_map/triangular_solve/custom-call.0 | solution.py:42
  745.7 0.5 fusion.30
  746.2 2.5 fusion.53
  748.7 8.1 all-gather.3
  756.8 1.1 reduce_sum.48
  757.9 1.3 convolution_multiply_fusion
  759.2 0.6 fusion.54
  759.8 10.6 %psum.31 = f32[16,8,8]{1,2,0:T(8,128)S(1)} all-reduce(f32[16,8,8]{1,2,0:T(8,128)S(1)} %fusion.54), channel_id=1, replica_groups=mesh['freq'=64,'inp'=4] {'inp'}, use_global_device_ids=true, to_apply=%region_9.12 | all-reduce | flops 1024 | bytes 8192 | tf_op jit(solution)/shard_map/psum | solution.py:40
  770.5 0.6 fusion.29
  771.2 12.4 %custom-call.18 = f32[16,8,8]{2,1,0:T(8,128)S(1)} custom-call(f32[16,8,8]{2,1,0:T(8,128)} %fusion.29), custom_call_target="Cholesky" | custom-call | tf_op jit(solution)/shard_map/jit(cholesky)/cholesky | solution.py:41
  783.8 10.0 %custom-call.19 = f32[16,1,8,8]{2,3,1,0:T(8,128)S(1)} custom-call(f32[16,1,8,8]{3,2,1,0:T(8,128)S(1)} %select_bitcast_fusion), custom_call_target="InvertDiagBlocksLowerTriangular" | custom-call | tf_op jit(solution)/shard_map/triangular_solve/custom-call.0 | solution.py:42
  793.8 0.5 fusion.27
  794.4 0.7 copy-done.1
  795.1 2.5 fusion.55
  797.6 8.3 %all-gather.4 = f32[64,8,192]{2,1,0:T(8,128)} all-gather(f32[16,8,192]{2,1,0:T(8,128)S(1)} %fusion.55), channel_id=6, replica_groups=mesh['freq'=64,'inp'=4] {'inp'}, dimensions={0}, use_global_device_ids=true | all-gather | bytes 491520 | tf_op jit(solution)/shard_map/all_gather | solution.py:11
  805.8 1.1 reduce_sum.49
  806.9 7.5 subtract_convert_fusion
  814.7 5.5 convert_element_type.82
  820.2 0.7 copy.99
  (37 shorter events, 3.3 us)
Async XLA Ops:
  0.6 15.1 %copy-start.2 = (f32[12,2048]{1,0:T(8,128)S(1)}, f32[12,2048]{1,0:T(8,128)}, u32[]{:S(2)}) copy-start(f32[12,2048]{1,0:T(8,128)} %param.7) | copy-start | bytes 294916
  4.0 193.6 %collective-permute-start.1 = (bf16[3,2048,256]{2,1,0:T(8,128)(2,1)S(1)}, bf16[3,2048,256]{2,1,0:T(8,128)(2,1)S(1)}, u32[]{:S(2)}, u32[]{:S(2)}) collective-permute-start(bf16[3,2048,256]{2,1,0:T(8,128)(2,1)S(1)} %convert_element_type.65), channel_id=1, source_target_pairs={{0,12},{4,16},{8,20},{12,24},{16,28},{20,32},{24,36},{28,40},{32,4... | collective-permute-start | bytes 9437192 | tf_op jit(solution)/shard_map/ppermute | solution.py:17
  9.0 205.7 %collective-permute-start.2 = (bf16[3,2048,256]{2,1,0:T(8,128)(2,1)S(1)}, bf16[3,2048,256]{2,1,0:T(8,128)(2,1)S(1)}, u32[]{:S(2)}, u32[]{:S(2)}) collective-permute-start(bf16[3,2048,256]{2,1,0:T(8,128)(2,1)S(1)} %convert_element_type.65), channel_id=1, source_target_pairs={{0,8},{4,12},{8,16},{12,20},{16,24},{20,28},{24,32},{28,36},{32,40... | collective-permute-start | bytes 9437192 | tf_op jit(solution)/shard_map/ppermute | solution.py:17
  10.6 275.1 %collective-permute-start.3 = (bf16[3,2048,256]{2,1,0:T(8,128)(2,1)S(1)}, bf16[3,2048,256]{2,1,0:T(8,128)(2,1)S(1)}, u32[]{:S(2)}, u32[]{:S(2)}) collective-permute-start(bf16[3,2048,256]{2,1,0:T(8,128)(2,1)S(1)} %convert_element_type.65), channel_id=1, source_target_pairs={{0,4},{4,8},{8,12},{12,16},{16,20},{20,24},{24,28},{28,32},{32,36}... | collective-permute-start | bytes 9437192 | tf_op jit(solution)/shard_map/ppermute | solution.py:17
  12.4 185.1 %collective-permute-start = (bf16[2,2048,256]{2,1,0:T(8,128)(2,1)S(1)}, bf16[2,2048,256]{2,1,0:T(8,128)(2,1)S(1)}, u32[]{:S(2)}, u32[]{:S(2)}) collective-permute-start(bf16[2,2048,256]{2,1,0:T(8,128)(2,1)S(1)} %slice.98), channel_id=1, source_target_pairs={{0,16},{4,20},{8,24},{12,28},{16,32},{20,36},{24,40},{28,44},{32,4... | collective-permute-start | bytes 6291464 | tf_op jit(solution)/shard_map/ppermute | solution.py:17
  295.7 64.8 %copy-start = (f32[3,2048,256]{2,1,0:T(8,128)S(1)}, f32[3,2048,256]{2,1,0:T(8,128)}, u32[]{:S(2)}) copy-start(f32[3,2048,256]{2,1,0:T(8,128)} %multiply_add_fusion) | copy-start | bytes 18874372
  418.7 170.6 %all-to-all-start = ((bf16[1024,3,2,256]{3,2,1,0:T(2,128)(2,1)}), bf16[1024,3,2,256]{3,2,1,0:T(2,128)(2,1)S(1)}, u32[]{:S(2)}, u32[]{:S(2)}) async-start(bf16[1024,3,2,256]{3,2,1,0:T(2,128)(2,1)} %copy.77), calls=%async_computation | async-start | bytes 6291456 | tf_op jit(solution)/shard_map/all_to_all | solution.py:92
  794.4 0.7 copy-start.1
